TPU v7x, 32 devices: a whole 2x2x4 slice. The times are simulated.
32 devices in a mesh: obs: 16 (over z, x, core), cell: 2 (over y).
Axes of the slice: x: 2, y: 2, z: 4, core: 2. Of those that a mesh axis runs over, the one named last changes fastest.
Arguments:
- flux_field: bfloat16 [2, 16, 64, 128], P('cell', 'obs'), may hold values from -6 to 6
- footprint: bfloat16 [256, 16, 128, 128], P('obs', 'cell'), may hold values from -0.125 to 0.125
- block_index: int32 [256, 16], P('obs', 'cell'), may hold values from 0 to 15
- tile_count: int32 [16], P('obs'), may hold values from 1 to 16, 128 in all
- sounding_week: int32 [256, 128], P('obs'), may hold values from 0 to 3
- member_ids: int32 [16], replicated, may hold values from 0 to 15, each once
- observed: float32 [256, 128], P('obs'), may hold values from -6 to 6
- perturb: bfloat16 [256, 16, 128], P('obs'), may hold values from -6 to 6
- obs_weight: float32 [256, 128], P('obs'), may hold values from 0.3 to 3
Outputs:
- gradient: float32 [2, 16, 64, 128], P('cell', 'obs')
- residual: bfloat16 [256, 16, 128], P('obs')
All inputs are finite; a program needn't handle non-finite values. No bound on the sum of `tile_count` on one device may be relied on, other than what follows from the above.
Results may differ from a plain program's by a relative error of at most 0.0028.
Values may be sent and summed in bfloat16 or wider, within the bound.
No kernel may reach another device: no remote copies, remote signals or barrier semaphores. Data moves between devices by JAX's collectives and lax.ppermute only.
A program may use at most 64 MiB of HBM per device.

v0:
```python
import jax
import jax.numpy as jnp
from jax import lax
from jax.sharding import PartitionSpec as P

MEMBERS = 16
WEEKS = 4


def weigh_misfit(modeled, alive, weights, seen, shifted):
    return (
        alive[:, None, None] * weights[:, None, :] * (modeled - seen[:, None, :] - shifted)
    ).astype(jnp.bfloat16)


def on_device(
    flux_field,
    footprint,
    block_index,
    tile_count,
    sounding_week,
    member_ids,
    observed,
    perturb,
    obs_weight,
):
    slab_rows = lax.all_gather(flux_field, "obs", axis=1, tiled=True)[0]
    slab_count = slab_rows.shape[0]
    slots = footprint.shape[0]
    sounds = footprint.shape[2]
    cells = footprint.shape[3]
    rows_all = WEEKS * MEMBERS
    chosen = slab_rows[block_index]
    mixing = jnp.einsum("tkrc,tksc->trs", chosen, footprint, preferred_element_type=jnp.float32)
    mixing = mixing.reshape(slots, WEEKS, MEMBERS, sounds)
    week_ids = jnp.arange(WEEKS, dtype=jnp.int32)
    week_hot = (sounding_week[:, None, :] == week_ids[None, :, None]).astype(jnp.float32)
    partial_value = jnp.einsum("twms,tws->tms", mixing, week_hot, precision=lax.Precision.HIGHEST)
    alive = (jnp.arange(slots, dtype=jnp.int32) < tile_count[0]).astype(jnp.float32)
    member_hot = (member_ids[:, None] == jnp.arange(MEMBERS, dtype=jnp.int32)[None, :]).astype(
        jnp.float32
    )
    shifted = jnp.einsum(
        "mk,tks->tms", member_hot, perturb.astype(jnp.float32), precision=lax.Precision.HIGHEST
    )
    modeled = lax.psum(partial_value, "cell")
    residual = weigh_misfit(modeled, alive, obs_weight, observed, shifted)
    week_mask = week_hot.astype(jnp.bfloat16)
    flat_blocks = block_index.reshape(-1)
    adjoint_rows = (residual[:, None, :, :] * week_mask[:, :, None, :]).reshape(
        slots, rows_all, sounds
    )
    contrib = jnp.einsum(
        "trs,tksc->tkrc", adjoint_rows, footprint, preferred_element_type=jnp.float32
    )
    partial_grad = jax.ops.segment_sum(
        contrib.reshape(-1, rows_all, cells), flat_blocks, num_segments=slab_count
    )
    gradient = lax.psum_scatter(partial_grad, "obs", scatter_dimension=0, tiled=True)
    return (gradient[None], residual)


def solution(mesh):
    return jax.shard_map(
        on_device,
        mesh=mesh,
        in_specs=(
            P("cell", "obs", None, None),
            P("obs", "cell", None, None),
            P("obs", "cell"),
            P("obs"),
            P("obs", None),
            P(),
            P("obs", None),
            P("obs", None, None),
            P("obs", None),
        ),
        out_specs=(P("cell", "obs", None, None), P("obs", None, None)),
        check_vma=False,
    )
```

profile of v0, /device:TPU:0, one launch (start us, length us, event | category | flops | bytes accessed | tf_op | source)
XLA Modules:
  0.0 140.3 jit_solution(12556074545440462448)
XLA Ops:
  7.2 0.0 copy-start
  7.2 0.0 all-reduce.2.cloned.1.call-start
  7.2 0.7 compare_select_fusion
  7.9 0.1 copy.17
  8.0 0.1 reshape.36
  8.1 0.7 fusion.4
  8.8 24.0 %all_gather.3 = bf16[1,16,64,128]{3,2,0,1:T(8,128)(2,1)S(1)} all-gather(bf16[1,1,64,128]{3,2,0,1:T(8,128)(2,1)} %bitcast.47), channel_id=1, replica_groups=mesh['obs'=16,'cell'=2] {'obs'}, dimensions={1}, use_global_device_ids=true | all-gather | bytes 278528 | tf_op jit(solution)/shard_map/all_gather | solution.py:27
  32.8 0.9 gather_fusion
  33.8 0.0 copy-start.3
  33.8 3.7 %fusion.8 = f32[16,64,128,1]{2,1,3,0:T(8,128)S(1)} fusion(bf16[16,8,64,128]{3,2,1,0:T(8,128)(2,1)S(1)} %bitcast.43, bf16[16,8,128,128]{3,2,1,0:T(8,128)(2,1)} %param.10), kind=kOutput, calls=%fused_computation.19 | convolution fusion | flops 268435456 | bytes 6815744 | tf_op jit(solution)/shard_map/tkrc,tksc->trs/dot_general | solution.py:34
  37.6 0.7 multiply_reduce_fusion
  38.3 0.0 all-reduce.2.cloned.1.call-update
  38.3 0.0 reduce-scatter.2.cloned.1.call-start
  38.4 0.1 copy.15
  39.1 0.1 reshape.44
  39.2 0.1 broadcast_multiply_fusion.1
  39.3 17.9 %all-reduce.2.cloned.1.call-done = f32[16,16,128]{2,1,0:T(8,128)} async-done(((f32[16,16,128]{2,1,0:T(8,128)}), f32[16,16,128]{2,1,0:T(8,128)}) %all-reduce.2.cloned.1.call-update) | async-done | bytes 131088 | tf_op jit(solution)/shard_map/psum | solution.py:46
  57.2 1.1 fusion.2
  58.3 0.0 copy-start.2
  58.4 4.8 %fusion.9 = f32[16,64,8,128]{3,1,2,0:T(8,128)} fusion(bf16[16,64,128,1]{2,1,3,0:T(8,128)(2,1)S(1)} %bitcast.45, bf16[16,8,128,128]{3,2,1,0:T(8,128)(2,1)} %param.10), kind=kOutput, calls=%fused_computation.20 | convolution fusion | flops 268435456 | bytes 8650752 | tf_op jit(solution)/shard_map/trs,tksc->tkrc/dot_general | solution.py:53
  63.3 13.5 %scatter_fusion = f32[16,64,128]{2,1,0:T(8,128)S(1)} fusion(f32[16,64,128]{2,1,0:T(8,128)S(1)} %broadcast_in_dim.6, s32[128]{0:T(128)S(1)} %reshape.44, f32[128,64,128]{2,1,0:T(8,128)} %bitcast.42), kind=kCustom, calls=%fused_computation.1 | custom fusion | flops 1048576 | bytes 12583424 | tf_op jit(solution)/shard_map/scatter-add | solution.py:56
  76.8 0.8 copy-done.1
  77.6 0.0 reduce-scatter.2.cloned.1.call-update
  77.6 55.9 %reduce-scatter.2.cloned.1.call-done = f32[1,64,128]{2,1,0:T(8,128)} async-done(((f32[16,64,128]{2,1,0:T(8,128)}), f32[1,64,128]{2,1,0:T(8,128)}) %reduce-scatter.2.cloned.1.call-update) | async-done | bytes 32784 | tf_op jit(solution)/shard_map/reduce_scatter | solution.py:59
  (14 shorter events, 0.1 us)
Async XLA Ops:
  7.2 50.0 %copy-start = (bf16[16,16,128]{2,1,0:T(8,128)(2,1)S(1)}, bf16[16,16,128]{2,1,0:T(8,128)(2,1)}, u32[]{:S(2)}) copy-start(bf16[16,16,128]{2,1,0:T(8,128)(2,1)} %param.16) | copy-start | bytes 196612
  7.2 50.0 %all-reduce.2.cloned.1.call-start = ((), (), s32[]{:S(2)}) async-start(), calls=%async_computation.1 | async-start | bytes 262144 | tf_op jit(solution)/shard_map/psum | solution.py:46
  33.8 4.6 %copy-start.3 = (s32[16,8]{0,1:T(8,128)S(1)}, s32[16,8]{0,1:T(8,128)}, u32[]{:S(2)}) copy-start(s32[16,8]{0,1:T(8,128)} %param.11) | copy-start | bytes 1540
  33.8 5.4 %copy-start.5 = (f32[16,128]{1,0:T(8,128)S(1)}, f32[16,128]{1,0:T(8,128)}, u32[]{:S(2)}) copy-start(f32[16,128]{1,0:T(8,128)} %param.17) | copy-start | bytes 24580
  33.8 23.4 %copy-start.4 = (f32[16,128]{1,0:T(8,128)S(1)}, f32[16,128]{1,0:T(8,128)}, u32[]{:S(2)}) copy-start(f32[16,128]{1,0:T(8,128)} %param.15) | copy-start | bytes 24580
  33.8 23.4 %copy-start.6 = (s32[16]{0:T(128)S(1)}, s32[16]{0:T(128)}, u32[]{:S(2)}) copy-start(s32[16]{0:T(128)} %param.14) | copy-start | bytes 196
  38.3 95.2 %reduce-scatter.2.cloned.1.call-start = ((), (), s32[]{:S(2)}) async-start(), calls=%async_computation.2 | async-start | bytes 557056 | tf_op jit(solution)/shard_map/reduce_scatter | solution.py:59
  58.3 4.9 %copy-start.2 = (bf16[16,16,128]{2,1,0:T(8,128)(2,1)}, bf16[16,16,128]{2,1,0:T(8,128)(2,1)S(1)}, u32[]{:S(2)}) copy-start(bf16[16,16,128]{2,1,0:T(8,128)(2,1)S(1)} %fusion.2) | copy-start | bytes 196612
  76.8 0.8 copy-start.1
Sparse Core Ops, SparseCore 0:
  38.4 18.7 all-reduce.1
  77.7 55.7 reduce-scatter.1
where the time goes:
time: 141 us; the launch traced here: 140 us
  waiting for transfers between devices  73.8 us (52%)
  blocking collectives  24 us (17%)
  other arithmetic  15.7 us (11%)
  between operations  14.8 us (10%)
  matrix products  9.68 us (7%)
  local copies, waits for them, and re-layouts  2.14 us (2%)
    reduce_scatter x1, waiting for transfers between devices, on_device(): lax.psum_scatter(partial_grad, 'obs', scatter_dimension=0, tiled=True)  55.9 us
    all_gather x1, blocking collectives, on_device(): slab_rows = lax.all_gather(flux_field, 'obs', axis=1, tiled=True)[0]  24 us
    psum x1, waiting for transfers between devices, on_device(): modeled = lax.psum(partial_value, 'cell')  17.9 us
    scatter-add x1, other arithmetic, on_device(): jax.ops.segment_sum(contrib.reshape(-1, rows_all, cells), flat_blocks, nu...  13.5 us
    dot_general x1, matrix products, on_device(): jnp.einsum('trs,tksc->tkrc', adjoint_rows, footprint, preferred_element_t...  4.84 us
    dot_general x1, matrix products, on_device(): jnp.einsum('tkrc,tksc->trs', chosen, footprint, preferred_element_type=jn...  3.73 us
  transfers between devices with their start and end apart: 2, of which 2 were waited for; matrix products, arithmetic and copies ran while one was open for 0% of the time, Pallas kernels for 0%

commit v1 on v0

--- a/solution.py
+++ b/solution.py
@@ -5,6 +5,19 @@
 
 MEMBERS = 16
 WEEKS = 4
+
+
+def ring_gather(x, axis, dim):
+    length, index, rows = (lax.axis_size(axis), lax.axis_index(axis), x.shape[dim])
+    right = [(i, (i + 1) % length) for i in range(length)]
+    out = jnp.zeros((*x.shape[:dim], length * rows, *x.shape[dim + 1 :]), x.dtype)
+    held = x
+    for lap in range(length):
+        owner = (index - lap) % length
+        out = lax.dynamic_update_slice_in_dim(out, held, owner * rows, axis=dim)
+        if lap < length - 1:
+            held = lax.ppermute(held, axis, right)
+    return out
 
 
 def weigh_misfit(modeled, alive, weights, seen, shifted):
@@ -24,7 +37,7 @@
     perturb,
     obs_weight,
 ):
-    slab_rows = lax.all_gather(flux_field, "obs", axis=1, tiled=True)[0]
+    slab_rows = ring_gather(flux_field, "obs", 1)[0]
     slab_count = slab_rows.shape[0]
     slots = footprint.shape[0]
     sounds = footprint.shape[2]

time: 141 us -> 205 us (1.45)
  waiting for transfers between devices: 73.8 us -> 160 us
  blocking collectives: 24 us -> 0 us
    ppermute x0 -> x15, waiting for transfers between devices: none -> 84.5 us  [ring_gather(): held = lax.ppermute(held, axis, right)]
    all_gather x1 -> x0, blocking collectives: 24 us -> none  [on_device(): slab_rows = lax.all_gather(flux_field, 'obs', axis=1, tiled=True)[0]]
  transfers between devices with their start and end apart: 2 -> 17, of which waited for: 2 -> 17; matrix products, arithmetic and copies ran while one was open for 0% -> 2% of each run, Pallas kernels for 0% -> 0%
where the time goes in v1:
time: 205 us; the launch traced here: 204 us
  waiting for transfers between devices  160 us (78%)
  other arithmetic  15.7 us (8%)
  between operations  14.9 us (7%)
  matrix products  9.71 us (5%)
  local copies, waits for them, and re-layouts  3.71 us (2%)
    ppermute x15, waiting for transfers between devices, ring_gather(): held = lax.ppermute(held, axis, right)  84.5 us
    reduce_scatter x1, waiting for transfers between devices, on_device(): lax.psum_scatter(partial_grad, 'obs', scatter_dimension=0, tiled=True)  55.9 us
    psum x1, waiting for transfers between devices, on_device(): modeled = lax.psum(partial_value, 'cell')  19.2 us
    scatter-add x1, other arithmetic, on_device(): jax.ops.segment_sum(contrib.reshape(-1, rows_all, cells), flat_blocks, nu...  13.5 us
    dot_general x1, matrix products, on_device(): jnp.einsum('trs,tksc->tkrc', adjoint_rows, footprint, preferred_element_t...  4.87 us
  transfers between devices with their start and end apart: 17, of which 17 were waited for; matrix products, arithmetic and copies ran while one was open for 2% of the time, Pallas kernels for 0%

profile of v1, /device:TPU:0, one launch (start us, length us, event | category | flops | bytes accessed | tf_op | source)
XLA Modules:
  0.0 204.3 jit_solution(3230963462496532788)
XLA Ops:
  10.8 0.8 copy.13
  11.7 2.6 %collective-permute-done = bf16[1,1,64,128]{3,2,1,0:T(8,128)(2,1)S(1)} collective-permute-done((bf16[1,1,64,128]{3,2,1,0:T(8,128)(2,1)}, bf16[1,1,64,128]{3,2,1,0:T(8,128)(2,1)S(1)}, u32[]{:S(2)}, u32[]{:S(2)}) %collective-permute-start) | collective-permute-done | bytes 16416 | tf_op jit(solution)/shard_map/ppermute | solution.py:19
  14.4 5.8 %collective-permute-done.1 = bf16[1,1,64,128]{3,2,1,0:T(8,128)(2,1)S(1)} collective-permute-done((bf16[1,1,64,128]{3,2,1,0:T(8,128)(2,1)S(1)}, bf16[1,1,64,128]{3,2,1,0:T(8,128)(2,1)S(1)}, u32[]{:S(2)}, u32[]{:S(2)}) %collective-permute-start.1) | collective-permute-done | bytes 16416 | tf_op jit(solution)/shard_map/ppermute | solution.py:19
  20.2 5.8 %collective-permute-done.2 = bf16[1,1,64,128]{3,2,1,0:T(8,128)(2,1)S(1)} collective-permute-done((bf16[1,1,64,128]{3,2,1,0:T(8,128)(2,1)S(1)}, bf16[1,1,64,128]{3,2,1,0:T(8,128)(2,1)S(1)}, u32[]{:S(2)}, u32[]{:S(2)}) %collective-permute-start.2) | collective-permute-done | bytes 16416 | tf_op jit(solution)/shard_map/ppermute | solution.py:19
  26.1 5.8 %collective-permute-done.3 = bf16[1,1,64,128]{3,2,1,0:T(8,128)(2,1)S(1)} collective-permute-done((bf16[1,1,64,128]{3,2,1,0:T(8,128)(2,1)S(1)}, bf16[1,1,64,128]{3,2,1,0:T(8,128)(2,1)S(1)}, u32[]{:S(2)}, u32[]{:S(2)}) %collective-permute-start.3) | collective-permute-done | bytes 16416 | tf_op jit(solution)/shard_map/ppermute | solution.py:19
  31.9 5.8 %collective-permute-done.4 = bf16[1,1,64,128]{3,2,1,0:T(8,128)(2,1)S(1)} collective-permute-done((bf16[1,1,64,128]{3,2,1,0:T(8,128)(2,1)S(1)}, bf16[1,1,64,128]{3,2,1,0:T(8,128)(2,1)S(1)}, u32[]{:S(2)}, u32[]{:S(2)}) %collective-permute-start.4) | collective-permute-done | bytes 16416 | tf_op jit(solution)/shard_map/ppermute | solution.py:19
  37.8 5.8 %collective-permute-done.5 = bf16[1,1,64,128]{3,2,1,0:T(8,128)(2,1)S(1)} collective-permute-done((bf16[1,1,64,128]{3,2,1,0:T(8,128)(2,1)S(1)}, bf16[1,1,64,128]{3,2,1,0:T(8,128)(2,1)S(1)}, u32[]{:S(2)}, u32[]{:S(2)}) %collective-permute-start.5) | collective-permute-done | bytes 16416 | tf_op jit(solution)/shard_map/ppermute | solution.py:19
  43.6 5.8 %collective-permute-done.6 = bf16[1,1,64,128]{3,2,1,0:T(8,128)(2,1)S(1)} collective-permute-done((bf16[1,1,64,128]{3,2,1,0:T(8,128)(2,1)S(1)}, bf16[1,1,64,128]{3,2,1,0:T(8,128)(2,1)S(1)}, u32[]{:S(2)}, u32[]{:S(2)}) %collective-permute-start.6) | collective-permute-done | bytes 16416 | tf_op jit(solution)/shard_map/ppermute | solution.py:19
  49.5 5.8 %collective-permute-done.7 = bf16[1,1,64,128]{3,2,1,0:T(8,128)(2,1)S(1)} collective-permute-done((bf16[1,1,64,128]{3,2,1,0:T(8,128)(2,1)S(1)}, bf16[1,1,64,128]{3,2,1,0:T(8,128)(2,1)S(1)}, u32[]{:S(2)}, u32[]{:S(2)}) %collective-permute-start.7) | collective-permute-done | bytes 16416 | tf_op jit(solution)/shard_map/ppermute | solution.py:19
  55.4 5.8 %collective-permute-done.8 = bf16[1,1,64,128]{3,2,1,0:T(8,128)(2,1)S(1)} collective-permute-done((bf16[1,1,64,128]{3,2,1,0:T(8,128)(2,1)S(1)}, bf16[1,1,64,128]{3,2,1,0:T(8,128)(2,1)S(1)}, u32[]{:S(2)}, u32[]{:S(2)}) %collective-permute-start.8) | collective-permute-done | bytes 16416 | tf_op jit(solution)/shard_map/ppermute | solution.py:19
  61.2 5.8 %collective-permute-done.9 = bf16[1,1,64,128]{3,2,1,0:T(8,128)(2,1)S(1)} collective-permute-done((bf16[1,1,64,128]{3,2,1,0:T(8,128)(2,1)S(1)}, bf16[1,1,64,128]{3,2,1,0:T(8,128)(2,1)S(1)}, u32[]{:S(2)}, u32[]{:S(2)}) %collective-permute-start.9) | collective-permute-done | bytes 16416 | tf_op jit(solution)/shard_map/ppermute | solution.py:19
  67.1 5.8 %collective-permute-done.10 = bf16[1,1,64,128]{3,2,1,0:T(8,128)(2,1)S(1)} collective-permute-done((bf16[1,1,64,128]{3,2,1,0:T(8,128)(2,1)S(1)}, bf16[1,1,64,128]{3,2,1,0:T(8,128)(2,1)S(1)}, u32[]{:S(2)}, u32[]{:S(2)}) %collective-permute-start.10) | collective-permute-done | bytes 16416 | tf_op jit(solution)/shard_map/ppermute | solution.py:19
  73.0 5.8 %collective-permute-done.11 = bf16[1,1,64,128]{3,2,1,0:T(8,128)(2,1)S(1)} collective-permute-done((bf16[1,1,64,128]{3,2,1,0:T(8,128)(2,1)S(1)}, bf16[1,1,64,128]{3,2,1,0:T(8,128)(2,1)S(1)}, u32[]{:S(2)}, u32[]{:S(2)}) %collective-permute-start.11) | collective-permute-done | bytes 16416 | tf_op jit(solution)/shard_map/ppermute | solution.py:19
  78.8 5.8 %collective-permute-done.12 = bf16[1,1,64,128]{3,2,1,0:T(8,128)(2,1)S(1)} collective-permute-done((bf16[1,1,64,128]{3,2,1,0:T(8,128)(2,1)S(1)}, bf16[1,1,64,128]{3,2,1,0:T(8,128)(2,1)S(1)}, u32[]{:S(2)}, u32[]{:S(2)}) %collective-permute-start.12) | collective-permute-done | bytes 16416 | tf_op jit(solution)/shard_map/ppermute | solution.py:19
  84.7 5.8 %collective-permute-done.13 = bf16[1,1,64,128]{3,2,1,0:T(8,128)(2,1)S(1)} collective-permute-done((bf16[1,1,64,128]{3,2,1,0:T(8,128)(2,1)S(1)}, bf16[1,1,64,128]{3,2,1,0:T(8,128)(2,1)S(1)}, u32[]{:S(2)}, u32[]{:S(2)}) %collective-permute-start.13) | collective-permute-done | bytes 16416 | tf_op jit(solution)/shard_map/ppermute | solution.py:19
  90.5 5.8 %collective-permute-done.14 = bf16[1,1,64,128]{3,2,1,0:T(8,128)(2,1)S(1)} collective-permute-done((bf16[1,1,64,128]{3,2,1,0:T(8,128)(2,1)S(1)}, bf16[1,1,64,128]{3,2,1,0:T(8,128)(2,1)S(1)}, u32[]{:S(2)}, u32[]{:S(2)}) %collective-permute-start.14) | collective-permute-done | bytes 16416 | tf_op jit(solution)/shard_map/ppermute | solution.py:19
  96.4 0.9 gather_fusion
  97.4 3.7 %fusion.8 = f32[16,64,128,1]{2,1,3,0:T(8,128)S(1)} fusion(bf16[16,8,64,128]{3,2,1,0:T(8,128)(2,1)S(1)} %bitcast.72, bf16[16,8,128,128]{3,2,1,0:T(8,128)(2,1)} %param.10), kind=kOutput, calls=%fused_computation.35 | convolution fusion | flops 268435456 | bytes 6815744 | tf_op jit(solution)/shard_map/tkrc,tksc->trs/dot_general | solution.py:47
  102.0 19.2 %all-reduce.2.cloned.1.call-done = f32[16,16,128]{2,1,0:T(8,128)} async-done(((f32[16,16,128]{2,1,0:T(8,128)}), f32[16,16,128]{2,1,0:T(8,128)}) %all-reduce.2.cloned.1.call-update) | async-done | bytes 131088 | tf_op jit(solution)/shard_map/psum | solution.py:59
  121.2 1.1 fusion.2
  122.3 4.9 %fusion.9 = f32[16,64,8,128]{3,1,2,0:T(8,128)} fusion(bf16[16,64,128,1]{2,1,3,0:T(8,128)(2,1)S(1)} %bitcast.74, bf16[16,8,128,128]{3,2,1,0:T(8,128)(2,1)} %param.10), kind=kOutput, calls=%fused_computation.36 | convolution fusion | flops 268435456 | bytes 8650752 | tf_op jit(solution)/shard_map/trs,tksc->tkrc/dot_general | solution.py:66
  127.3 13.5 %scatter_fusion = f32[16,64,128]{2,1,0:T(8,128)S(1)} fusion(f32[16,64,128]{2,1,0:T(8,128)S(1)} %broadcast_in_dim.6, s32[128]{0:T(128)S(1)} %reshape.76, f32[128,64,128]{2,1,0:T(8,128)} %bitcast.71), kind=kCustom, calls=%fused_computation.1 | custom fusion | flops 1048576 | bytes 12583424 | tf_op jit(solution)/shard_map/scatter-add | solution.py:69
  140.8 0.8 copy-done.1
  141.6 55.9 %reduce-scatter.2.cloned.1.call-done = f32[1,64,128]{2,1,0:T(8,128)} async-done(((f32[16,64,128]{2,1,0:T(8,128)}), f32[1,64,128]{2,1,0:T(8,128)}) %reduce-scatter.2.cloned.1.call-update) | async-done | bytes 32784 | tf_op jit(solution)/shard_map/reduce_scatter | solution.py:72
  (58 shorter events, 4.1 us)
Async XLA Ops:
  7.2 114.0 %copy-start = (bf16[16,16,128]{2,1,0:T(8,128)(2,1)S(1)}, bf16[16,16,128]{2,1,0:T(8,128)(2,1)}, u32[]{:S(2)}) copy-start(bf16[16,16,128]{2,1,0:T(8,128)(2,1)} %param.16) | copy-start | bytes 196612
  7.2 114.0 %all-reduce.2.cloned.1.call-start = ((), (), s32[]{:S(2)}) async-start(), calls=%async_computation.1 | async-start | bytes 262144 | tf_op jit(solution)/shard_map/psum | solution.py:59
  7.2 7.1 %collective-permute-start = (bf16[1,1,64,128]{3,2,1,0:T(8,128)(2,1)}, bf16[1,1,64,128]{3,2,1,0:T(8,128)(2,1)S(1)}, u32[]{:S(2)}, u32[]{:S(2)}) collective-permute-start(bf16[1,1,64,128]{3,2,1,0:T(8,128)(2,1)} %param.9), channel_id=1, source_target_pairs={{0,2},{2,4},{4,6},{6,8},{8,10},{10,12},{12,14},{14,16},{16,18},{18... | collective-permute-start | bytes 49160 | tf_op jit(solution)/shard_map/ppermute | solution.py:19
  14.3 5.9 %collective-permute-start.1 = (bf16[1,1,64,128]{3,2,1,0:T(8,128)(2,1)S(1)}, bf16[1,1,64,128]{3,2,1,0:T(8,128)(2,1)S(1)}, u32[]{:S(2)}, u32[]{:S(2)}) collective-permute-start(bf16[1,1,64,128]{3,2,1,0:T(8,128)(2,1)S(1)} %collective-permute-done), channel_id=1, source_target_pairs={{0,2},{2,4},{4,6},{6,8},{8,10},{10,12},{12,14},{14,16},{16,18},{18... | collective-permute-start | bytes 49160 | tf_op jit(solution)/shard_map/ppermute | solution.py:19
  20.2 5.9 %collective-permute-start.2 = (bf16[1,1,64,128]{3,2,1,0:T(8,128)(2,1)S(1)}, bf16[1,1,64,128]{3,2,1,0:T(8,128)(2,1)S(1)}, u32[]{:S(2)}, u32[]{:S(2)}) collective-permute-start(bf16[1,1,64,128]{3,2,1,0:T(8,128)(2,1)S(1)} %collective-permute-done.1), channel_id=1, source_target_pairs={{0,2},{2,4},{4,6},{6,8},{8,10},{10,12},{12,14},{14,16},{16,18},{18... | collective-permute-start | bytes 49160 | tf_op jit(solution)/shard_map/ppermute | solution.py:19
  26.1 5.9 %collective-permute-start.3 = (bf16[1,1,64,128]{3,2,1,0:T(8,128)(2,1)S(1)}, bf16[1,1,64,128]{3,2,1,0:T(8,128)(2,1)S(1)}, u32[]{:S(2)}, u32[]{:S(2)}) collective-permute-start(bf16[1,1,64,128]{3,2,1,0:T(8,128)(2,1)S(1)} %collective-permute-done.2), channel_id=1, source_target_pairs={{0,2},{2,4},{4,6},{6,8},{8,10},{10,12},{12,14},{14,16},{16,18},{18... | collective-permute-start | bytes 49160 | tf_op jit(solution)/shard_map/ppermute | solution.py:19
  31.9 5.9 %collective-permute-start.4 = (bf16[1,1,64,128]{3,2,1,0:T(8,128)(2,1)S(1)}, bf16[1,1,64,128]{3,2,1,0:T(8,128)(2,1)S(1)}, u32[]{:S(2)}, u32[]{:S(2)}) collective-permute-start(bf16[1,1,64,128]{3,2,1,0:T(8,128)(2,1)S(1)} %collective-permute-done.3), channel_id=1, source_target_pairs={{0,2},{2,4},{4,6},{6,8},{8,10},{10,12},{12,14},{14,16},{16,18},{18... | collective-permute-start | bytes 49160 | tf_op jit(solution)/shard_map/ppermute | solution.py:19
  37.8 5.9 %collective-permute-start.5 = (bf16[1,1,64,128]{3,2,1,0:T(8,128)(2,1)S(1)}, bf16[1,1,64,128]{3,2,1,0:T(8,128)(2,1)S(1)}, u32[]{:S(2)}, u32[]{:S(2)}) collective-permute-start(bf16[1,1,64,128]{3,2,1,0:T(8,128)(2,1)S(1)} %collective-permute-done.4), channel_id=1, source_target_pairs={{0,2},{2,4},{4,6},{6,8},{8,10},{10,12},{12,14},{14,16},{16,18},{18... | collective-permute-start | bytes 49160 | tf_op jit(solution)/shard_map/ppermute | solution.py:19
  43.6 5.9 %collective-permute-start.6 = (bf16[1,1,64,128]{3,2,1,0:T(8,128)(2,1)S(1)}, bf16[1,1,64,128]{3,2,1,0:T(8,128)(2,1)S(1)}, u32[]{:S(2)}, u32[]{:S(2)}) collective-permute-start(bf16[1,1,64,128]{3,2,1,0:T(8,128)(2,1)S(1)} %collective-permute-done.5), channel_id=1, source_target_pairs={{0,2},{2,4},{4,6},{6,8},{8,10},{10,12},{12,14},{14,16},{16,18},{18... | collective-permute-start | bytes 49160 | tf_op jit(solution)/shard_map/ppermute | solution.py:19
  49.5 5.9 %collective-permute-start.7 = (bf16[1,1,64,128]{3,2,1,0:T(8,128)(2,1)S(1)}, bf16[1,1,64,128]{3,2,1,0:T(8,128)(2,1)S(1)}, u32[]{:S(2)}, u32[]{:S(2)}) collective-permute-start(bf16[1,1,64,128]{3,2,1,0:T(8,128)(2,1)S(1)} %collective-permute-done.6), channel_id=1, source_target_pairs={{0,2},{2,4},{4,6},{6,8},{8,10},{10,12},{12,14},{14,16},{16,18},{18... | collective-permute-start | bytes 49160 | tf_op jit(solution)/shard_map/ppermute | solution.py:19
  55.4 5.9 %collective-permute-start.8 = (bf16[1,1,64,128]{3,2,1,0:T(8,128)(2,1)S(1)}, bf16[1,1,64,128]{3,2,1,0:T(8,128)(2,1)S(1)}, u32[]{:S(2)}, u32[]{:S(2)}) collective-permute-start(bf16[1,1,64,128]{3,2,1,0:T(8,128)(2,1)S(1)} %collective-permute-done.7), channel_id=1, source_target_pairs={{0,2},{2,4},{4,6},{6,8},{8,10},{10,12},{12,14},{14,16},{16,18},{18... | collective-permute-start | bytes 49160 | tf_op jit(solution)/shard_map/ppermute | solution.py:19
  61.2 5.9 %collective-permute-start.9 = (bf16[1,1,64,128]{3,2,1,0:T(8,128)(2,1)S(1)}, bf16[1,1,64,128]{3,2,1,0:T(8,128)(2,1)S(1)}, u32[]{:S(2)}, u32[]{:S(2)}) collective-permute-start(bf16[1,1,64,128]{3,2,1,0:T(8,128)(2,1)S(1)} %collective-permute-done.8), channel_id=1, source_target_pairs={{0,2},{2,4},{4,6},{6,8},{8,10},{10,12},{12,14},{14,16},{16,18},{18... | collective-permute-start | bytes 49160 | tf_op jit(solution)/shard_map/ppermute | solution.py:19
  67.1 5.9 %collective-permute-start.10 = (bf16[1,1,64,128]{3,2,1,0:T(8,128)(2,1)S(1)}, bf16[1,1,64,128]{3,2,1,0:T(8,128)(2,1)S(1)}, u32[]{:S(2)}, u32[]{:S(2)}) collective-permute-start(bf16[1,1,64,128]{3,2,1,0:T(8,128)(2,1)S(1)} %collective-permute-done.9), channel_id=1, source_target_pairs={{0,2},{2,4},{4,6},{6,8},{8,10},{10,12},{12,14},{14,16},{16,18},{18... | collective-permute-start | bytes 49160 | tf_op jit(solution)/shard_map/ppermute | solution.py:19
  72.9 5.9 %collective-permute-start.11 = (bf16[1,1,64,128]{3,2,1,0:T(8,128)(2,1)S(1)}, bf16[1,1,64,128]{3,2,1,0:T(8,128)(2,1)S(1)}, u32[]{:S(2)}, u32[]{:S(2)}) collective-permute-start(bf16[1,1,64,128]{3,2,1,0:T(8,128)(2,1)S(1)} %collective-permute-done.10), channel_id=1, source_target_pairs={{0,2},{2,4},{4,6},{6,8},{8,10},{10,12},{12,14},{14,16},{16,18},{18... | collective-permute-start | bytes 49160 | tf_op jit(solution)/shard_map/ppermute | solution.py:19
  78.8 5.9 %collective-permute-start.12 = (bf16[1,1,64,128]{3,2,1,0:T(8,128)(2,1)S(1)}, bf16[1,1,64,128]{3,2,1,0:T(8,128)(2,1)S(1)}, u32[]{:S(2)}, u32[]{:S(2)}) collective-permute-start(bf16[1,1,64,128]{3,2,1,0:T(8,128)(2,1)S(1)} %collective-permute-done.11), channel_id=1, source_target_pairs={{0,2},{2,4},{4,6},{6,8},{8,10},{10,12},{12,14},{14,16},{16,18},{18... | collective-permute-start | bytes 49160 | tf_op jit(solution)/shard_map/ppermute | solution.py:19
  84.7 5.9 %collective-permute-start.13 = (bf16[1,1,64,128]{3,2,1,0:T(8,128)(2,1)S(1)}, bf16[1,1,64,128]{3,2,1,0:T(8,128)(2,1)S(1)}, u32[]{:S(2)}, u32[]{:S(2)}) collective-permute-start(bf16[1,1,64,128]{3,2,1,0:T(8,128)(2,1)S(1)} %collective-permute-done.12), channel_id=1, source_target_pairs={{0,2},{2,4},{4,6},{6,8},{8,10},{10,12},{12,14},{14,16},{16,18},{18... | collective-permute-start | bytes 49160 | tf_op jit(solution)/shard_map/ppermute | solution.py:19
  90.5 5.9 %collective-permute-start.14 = (bf16[1,1,64,128]{3,2,1,0:T(8,128)(2,1)S(1)}, bf16[1,1,64,128]{3,2,1,0:T(8,128)(2,1)S(1)}, u32[]{:S(2)}, u32[]{:S(2)}) collective-permute-start(bf16[1,1,64,128]{3,2,1,0:T(8,128)(2,1)S(1)} %collective-permute-done.13), channel_id=1, source_target_pairs={{0,2},{2,4},{4,6},{6,8},{8,10},{10,12},{12,14},{14,16},{16,18},{18... | collective-permute-start | bytes 49160 | tf_op jit(solution)/shard_map/ppermute | solution.py:19
  97.4 4.5 %copy-start.4 = (f32[16,128]{1,0:T(8,128)S(1)}, f32[16,128]{1,0:T(8,128)}, u32[]{:S(2)}) copy-start(f32[16,128]{1,0:T(8,128)} %param.17) | copy-start | bytes 24580
  97.4 23.8 %copy-start.3 = (f32[16,128]{1,0:T(8,128)S(1)}, f32[16,128]{1,0:T(8,128)}, u32[]{:S(2)}) copy-start(f32[16,128]{1,0:T(8,128)} %param.15) | copy-start | bytes 24580
  97.4 23.8 %copy-start.5 = (s32[16]{0:T(128)S(1)}, s32[16]{0:T(128)}, u32[]{:S(2)}) copy-start(s32[16]{0:T(128)} %param.14) | copy-start | bytes 196
  101.8 95.6 %reduce-scatter.2.cloned.1.call-start = ((), (), s32[]{:S(2)}) async-start(), calls=%async_computation.2 | async-start | bytes 557056 | tf_op jit(solution)/shard_map/reduce_scatter | solution.py:72
  122.3 4.9 %copy-start.2 = (bf16[16,16,128]{2,1,0:T(8,128)(2,1)}, bf16[16,16,128]{2,1,0:T(8,128)(2,1)S(1)}, u32[]{:S(2)}) copy-start(bf16[16,16,128]{2,1,0:T(8,128)(2,1)S(1)} %fusion.2) | copy-start | bytes 196612
  140.8 0.8 copy-start.1
Sparse Core Ops, SparseCore 0:
  102.0 19.1 all-reduce.1
  141.7 55.7 reduce-scatter.1
